TPU v7x, 32 devices: a whole 2x2x4 slice. The times are simulated.
32 devices in a mesh: date: 2 (over x), strip: 16 (over z, y, core).
Axes of the slice: x: 2, y: 2, z: 4, core: 2. Of those that a mesh axis runs over, the one named last changes fastest.
Arguments:
- slc: bfloat16 [20, 2, 192, 1408], P('date', None, 'strip'), may hold values from -60 to 60
Outputs:
- coherence: float32 [20, 20, 2, 64, 128], P('date', None, None, 'strip')
All inputs are finite; a program needn't handle non-finite values.
Results may differ from a plain program's by a relative error of at most 0.0003.
Values may be sent and summed in bfloat16 or wider, within the bound.
No kernel may reach another device: no remote copies, remote signals or barrier semaphores. Data moves between devices by JAX's collectives and lax.ppermute only.
A program may use at most 128 MiB of HBM per device.

v0:
```python
import jax
import jax.numpy as jnp
from jax import lax
from jax.sharding import PartitionSpec as P

EPS = 1e-06


def with_halo(cells, sides, width):
    for axis, dim in sides:
        count = lax.axis_size(axis)
        ends = count - 1
        head = lax.slice_in_dim(cells, 0, width, axis=dim)
        tail = lax.slice_in_dim(cells, cells.shape[dim] - width, cells.shape[dim], axis=dim)
        cells = jnp.concatenate(
            [
                lax.ppermute(tail, axis, [(i, (i + 1) % count) for i in range(ends)]),
                cells,
                lax.ppermute(head, axis, [((i + 1) % count, i) for i in range(ends)]),
            ],
            axis=dim,
        )
    return cells


def cell_layout(block):
    shape = block.shape
    return block.reshape((shape[0], 2, shape[2] // 3, 3, shape[3] // 11, 11))


def boxcar(cells):
    padded = jnp.pad(cells, [(0, 0)] * (cells.ndim - 1) + [(1, 1)])
    tri = padded[..., :-2] + padded[..., 1:-1] + padded[..., 2:]
    return tri[..., :-2, :] + tri[..., 1:-1, :] + tri[..., 2:, :]


def amplitude(cells_bf):
    values = cells_bf.astype(jnp.float32)
    power = jnp.sum(values * values, axis=(1, 3, 5))
    return lax.rsqrt(boxcar(power) + EPS)


def pair_terms(own_cells, own_scale, other_cells, other_scale):
    sums = lax.dot_general(
        own_cells,
        other_cells,
        (((3, 5), (3, 5)), ((2, 4), (2, 4))),
        preferred_element_type=jnp.float32,
    )
    first = sums[:, :, :, 0, :, 0] + sums[:, :, :, 1, :, 1]
    second = sums[:, :, :, 1, :, 0] - sums[:, :, :, 0, :, 1]
    both = jnp.stack([first, second], axis=4)
    both = jnp.transpose(both, (2, 3, 4, 0, 1))
    return boxcar(both) * (own_scale[:, None] * other_scale[None])[:, :, None]


def per_device(slc):
    local_dates = slc.shape[0]
    whole = lax.all_gather(slc, "date", axis=0, tiled=True)
    padded = with_halo(whole, (("strip", 2),), 3)
    all_cells = cell_layout(padded)
    all_scale = amplitude(all_cells)
    first_date = lax.axis_index("date") * local_dates
    own_cells = lax.dynamic_slice_in_dim(all_cells, first_date, local_dates, 0)
    own_scale = lax.dynamic_slice_in_dim(all_scale, first_date, local_dates, 0)
    return pair_terms(own_cells, own_scale, all_cells, all_scale)


def solution(mesh):
    return jax.shard_map(
        per_device,
        mesh=mesh,
        in_specs=(P("date", None, "strip", None),),
        out_specs=P("date", None, None, "strip", None),
        check_vma=False,
    )
```

profile of v0, /device:TPU:5, one launch (start us, length us, event | category | flops | bytes accessed | tf_op | source)
XLA Modules:
  0.0 243.3 jit_solution(3144084779581970662)
XLA Ops:
  6.5 0.0 all-gather.2.cloned.1.call-start
  6.5 0.7 all-gather.2.cloned.1.call-update
  7.3 27.6 %all-gather.2.cloned.1.call-done = bf16[20,2,12,1408]{3,1,2,0:T(2,128)(2,1)} async-done(((bf16[10,2,12,1408]{3,1,2,0:T(2,128)(2,1)}), bf16[20,2,12,1408]{3,1,2,0:T(2,128)(2,1)}) %all-gather.2.cloned.1.call-update) | async-done | bytes 1351696 | tf_op jit(solution)/shard_map/all_gather | solution.py:59
  34.9 0.0 copy-start.1
  34.9 1.7 fusion.14
  36.5 3.7 %collective-permute-start = (bf16[20,2,3,1408]{3,1,2,0:T(2,128)(2,1)S(1)}, bf16[20,2,3,1408]{3,1,2,0:T(2,128)(2,1)S(1)}, u32[]{:S(2)}, u32[]{:S(2)}) collective-permute-start(bf16[20,2,3,1408]{3,1,2,0:T(2,128)(2,1)S(1)} %get-tuple-element.8), channel_id=1, source_target_pairs={{0,1},{1,2},{2,3},{3,4},{4,5},{5,6},{6,7},{7,8},{8,9},{9,10},{10,1... | collective-permute-start | bytes 1013768 | tf_op jit(solution)/shard_map/ppermute | solution.py:17
  40.2 1.9 collective-permute-start.1
  42.1 2.2 collective-permute-done
  44.3 0.2 constant_dynamic-update-slice_fusion.2
  44.5 0.0 copy-done.1
  44.5 1.1 constant_dynamic-update-slice_fusion.1
  45.6 4.0 %collective-permute-done.1 = bf16[20,2,3,1408]{3,1,2,0:T(2,128)(2,1)S(1)} collective-permute-done((bf16[20,2,3,1408]{3,1,2,0:T(2,128)(2,1)S(1)}, bf16[20,2,3,1408]{3,1,2,0:T(2,128)(2,1)S(1)}, u32[]{:S(2)}, u32[]{:S(2)}) %collective-permute-start.1) | collective-permute-done | bytes 337952 | tf_op jit(solution)/shard_map/ppermute | solution.py:19
  49.6 0.3 constant_dynamic-update-slice_fusion
  49.9 0.0 copy-start
  49.9 1.3 copy-done
  51.2 5.4 %multiply_reduce_fusion = f32[20,18,1408]{2,1,0:T(8,128)S(1)} fusion(bf16[20,2,18,1408]{3,1,2,0:T(2,128)(2,1)S(1)} %constant_dynamic-update-slice_fusion), kind=kLoop, calls=%fused_computation.8 | loop fusion | flops 2534400 | bytes 4055040 | tf_op jit(solution)/shard_map/reduce_sum | solution.py:39
  56.6 55.1 %reshape.43 = bf16[20,2,6,3,128,11]{5,4,1,3,2,0:T(8,128)(2,1)} reshape(bf16[20,2,18,1408]{3,1,2,0:T(2,128)(2,1)} %copy-done) | data formatting | bytes 4055040 | tf_op jit(solution)/shard_map/reshape | solution.py:28
  111.7 1.8 copy.15
  113.5 26.9 %reduce_sum.14 = f32[20,6,3,128,11]{4,3,0,2,1:T(8,128)} reshape(f32[20,18,1408]{2,0,1:T(8,128)} %copy.15) | data formatting | bytes 4055040 | tf_op jit(solution)/shard_map/reduce_sum | solution.py:39
  140.4 9.3 %reduce_sum.18 = f32[20,6,128]{2,0,1:T(8,128)S(1)} reduce(f32[20,6,3,128,11]{4,3,0,2,1:T(8,128)} %reduce_sum.14, f32[]{:T(128)} %constant.15.clone.1), dimensions={2,4}, to_apply=%region_1.2 | reduce | flops 491520 | bytes 2088964 | tf_op jit(solution)/shard_map/reduce_sum | solution.py:39
  149.7 0.1 fusion.11
  149.9 11.3 %constant_dynamic-slice_fusion.1 = bf16[10,2,6,3,128,11]{5,4,1,3,2,0:T(8,128)(2,1)} fusion(bf16[20,2,6,3,128,11]{5,4,1,3,2,0:T(8,128)(2,1)} %reshape.43, s32[]{:T(128)S(6)} %select_n.4), kind=kLoop, calls=%fused_computation.30 | loop fusion | bytes 2027524 | tf_op jit(solution)/shard_map/dynamic_slice | solution.py:64
  161.2 45.5 %fusion.2 = f32[6,128,10,2,20,2]{4,2,5,3,1,0:T(8,128)} fusion(bf16[20,2,6,3,128,11,1]{5,4,1,3,2,0,6:T(8,128)(2,1)} %bitcast.21, bf16[10,2,6,3,128,11]{5,4,1,3,2,0:T(8,128)(2,1)} %constant_dynamic-slice_fusion.1), kind=kOutput, calls=%fused_computation.3 | convolution fusion | flops 40550400 | bytes 5498880 | tf_op jit(solution)/shard_map/dot_general | solution.py:44
  206.7 14.2 %fusion.6 = (f32[6,128,10,20,1]{3,2,1,0,4:T(8,128)}, f32[6,128,10,20,1]{3,2,1,0,4:T(8,128)}) fusion(f32[6,128,10,2,20,2]{4,2,5,3,1,0:T(8,128)} %fusion.2), kind=kLoop, calls=%fused_computation.7 | loop fusion | flops 307200 | bytes 3686400 | tf_op jit(solution)/shard_map/add | solution.py:50
  220.8 5.0 %copy.13 = f32[6,128,10,20,1]{1,4,3,2,0:T(1,128)S(1)} copy(f32[6,128,10,20,1]{3,2,1,0,4:T(8,128)} %get-tuple-element.5) | data formatting | bytes 1228800 | tf_op jit(solution)/shard_map/add | solution.py:50
  225.8 5.2 %copy.14 = f32[6,128,10,20,1]{1,4,3,2,0:T(1,128)S(1)} copy(f32[6,128,10,20,1]{3,2,1,0,4:T(8,128)} %get-tuple-element.6) | data formatting | bytes 1228800 | tf_op jit(solution)/shard_map/sub | solution.py:51
  231.0 1.1 maximum_bitcast_fusion
  232.1 2.6 %fusion.8 = f32[10,20,2,6,128]{4,2,1,0,3:T(2,128)S(1)} fusion(f32[10,20,2,6,128]{4,2,1,0,3:T(2,128)S(1)} %maximum_bitcast_fusion), kind=kLoop, calls=%fused_computation.12 | loop fusion | flops 614400 | bytes 2457600 | tf_op jit(solution)/shard_map/add | solution.py:33
  234.7 0.5 fusion.9
  235.3 1.2 copy.16
  (3 shorter events, 0.1 us)
Async XLA Ops:
  6.5 28.3 %all-gather.2.cloned.1.call-start = ((), (), s32[]{:S(2)}) async-start(), calls=%async_computation | async-start | bytes 2027520 | tf_op jit(solution)/shard_map/all_gather | solution.py:59
  34.9 9.7 %copy-start.1 = (bf16[20,2,12,1408]{3,1,2,0:T(2,128)(2,1)S(1)}, bf16[20,2,12,1408]{3,1,2,0:T(2,128)(2,1)}, u32[]{:S(2)}) copy-start(bf16[20,2,12,1408]{3,1,2,0:T(2,128)(2,1)} %all-gather.2.cloned.1.call-done) | copy-start | bytes 4055044
  36.5 7.8 %collective-permute-start = (bf16[20,2,3,1408]{3,1,2,0:T(2,128)(2,1)S(1)}, bf16[20,2,3,1408]{3,1,2,0:T(2,128)(2,1)S(1)}, u32[]{:S(2)}, u32[]{:S(2)}) collective-permute-start(bf16[20,2,3,1408]{3,1,2,0:T(2,128)(2,1)S(1)} %get-tuple-element.8), channel_id=1, source_target_pairs={{0,1},{1,2},{2,3},{3,4},{4,5},{5,6},{6,7},{7,8},{8,9},{9,10},{10,1... | collective-permute-start | bytes 1013768 | tf_op jit(solution)/shard_map/ppermute | solution.py:17
  40.2 9.4 %collective-permute-start.1 = (bf16[20,2,3,1408]{3,1,2,0:T(2,128)(2,1)S(1)}, bf16[20,2,3,1408]{3,1,2,0:T(2,128)(2,1)S(1)}, u32[]{:S(2)}, u32[]{:S(2)}) collective-permute-start(bf16[20,2,3,1408]{3,1,2,0:T(2,128)(2,1)S(1)} %get-tuple-element.7), channel_id=1, source_target_pairs={{1,0},{2,1},{3,2},{4,3},{5,4},{6,5},{7,6},{8,7},{9,8},{10,9},{11,1... | collective-permute-start | bytes 1013768 | tf_op jit(solution)/shard_map/ppermute | solution.py:19
  49.9 1.3 copy-start
Sparse Core Ops, SparseCore 0:
  8.9 25.9 all-gather.1
where the time goes:
time: 244 us; the launch traced here: 243 us
  local copies, waits for them, and re-layouts  111 us (45%)
  matrix products  45.5 us (19%)
  waiting for transfers between devices  34.5 us (14%)
  other arithmetic  33.2 us (14%)
  between operations  13.5 us (6%)
  starting transfers between devices  5.59 us (2%)
    reshape x1, local copies, waits for them, and re-layouts, cell_layout(): return block.reshape((shape[0], 2, shape[2] // 3, 3, shape[3] // 11, 11))  55.1 us
    dot_general x1, matrix products, pair_terms(): lax.dot_general(own_cells, other_cells, (((3, 5), (3, 5)), ((2, 4), (2, 4...  45.5 us
    reduce_sum x2, local copies, waits for them, and re-layouts, amplitude(): power = jnp.sum(values * values, axis=(1, 3, 5))  28.7 us
    all_gather x1, waiting for transfers between devices, per_device(): whole = lax.all_gather(slc, 'date', axis=0, tiled=True)  27.6 us
    reduce_sum x2, other arithmetic, amplitude(): power = jnp.sum(values * values, axis=(1, 3, 5))  14.7 us
    add x1, other arithmetic, pair_terms(): first = sums[:, :, :, 0, :, 0] + sums[:, :, :, 1, :, 1]  14.2 us
    dynamic_slice x1, local copies, waits for them, and re-layouts, per_device(): own_cells = lax.dynamic_slice_in_dim(all_cells, first_date, local_dates, 0)  11.3 us
    sub x1, local copies, waits for them, and re-layouts, pair_terms(): second = sums[:, :, :, 1, :, 0] - sums[:, :, :, 0, :, 1]  5.2 us
  transfers between devices with their start and end apart: 3, of which 3 were waited for; matrix products, arithmetic and copies ran while one was open for 1% of the time, Pallas kernels for 0%

commit v1 on v0

--- a/solution.py
+++ b/solution.py
@@ -56,7 +56,15 @@
 
 def per_device(slc):
     local_dates = slc.shape[0]
-    whole = lax.all_gather(slc, "date", axis=0, tiled=True)
+    w2, outer, p_next = (lax.axis_size("date"), lax.axis_index("date"), slc.shape[0])
+    reply, finding = (slc, 1)
+    while finding < w2:
+        gallery = []
+        for j0 in tuple(range(w2)):
+            gallery.append((j0, (j0 - finding) % w2))
+        reply = jnp.concatenate([reply, lax.ppermute(reply, "date", gallery)], axis=0)
+        finding = 2 * finding
+    whole = jnp.roll(reply, shift=outer * p_next, axis=0)
     padded = with_halo(whole, (("strip", 2),), 3)
     all_cells = cell_layout(padded)
     all_scale = amplitude(all_cells)

time: 244 us -> 221 us (0.906)
  between operations: 13.5 us -> 0.13 us
  waiting for transfers between devices: 34.5 us -> 22.5 us
  other arithmetic: 33.2 us -> 41.3 us
  local copies, waits for them, and re-layouts: 111 us -> 104 us
    all_gather x1 -> x0, waiting for transfers between devices: 27.6 us -> none  [per_device(): whole = lax.all_gather(slc, 'date', axis=0, tiled=True)]
    ppermute x0 -> x1, waiting for transfers between devices: none -> 15 us  [per_device(): lax.ppermute(reply, 'date', gallery)]
    concatenate x0 -> x1, other arithmetic: none -> 6.57 us  [per_device(): whole = jnp.roll(reply, shift=outer * p_next, axis=0)]
    unnamed x6 -> x2, local copies, waits for them, and re-layouts: 2.63 us -> 0.01 us
  transfers between devices with their start and end apart: 3 -> 3, of which waited for: 3 -> 3; matrix products, arithmetic and copies ran while one was open for 1% -> 0% of each run, Pallas kernels for 0% -> 0%
where the time goes in v1:
time: 221 us
  local copies, waits for them, and re-layouts  104 us (47%)
  matrix products  45.5 us (21%)
  other arithmetic  41.3 us (19%)
  waiting for transfers between devices  22.5 us (10%)
  starting transfers between devices  7.71 us (3%)
    reshape x1, local copies, waits for them, and re-layouts, cell_layout(): return block.reshape((shape[0], 2, shape[2] // 3, 3, shape[3] // 11, 11))  54 us
    dot_general x1, matrix products, pair_terms(): lax.dot_general(own_cells, other_cells, (((3, 5), (3, 5)), ((2, 4), (2, 4...  45.5 us
    reduce_sum x2, local copies, waits for them, and re-layouts, amplitude(): power = jnp.sum(values * values, axis=(1, 3, 5))  26.4 us
    reduce_sum x2, other arithmetic, amplitude(): power = jnp.sum(values * values, axis=(1, 3, 5))  16.2 us
    ppermute x1, waiting for transfers between devices, per_device(): lax.ppermute(reply, 'date', gallery)  15 us
    add x1, other arithmetic, pair_terms(): first = sums[:, :, :, 0, :, 0] + sums[:, :, :, 1, :, 1]  14.1 us
    dynamic_slice x1, local copies, waits for them, and re-layouts, per_device(): own_cells = lax.dynamic_slice_in_dim(all_cells, first_date, local_dates, 0)  11.3 us
    concatenate x1, other arithmetic, per_device(): whole = jnp.roll(reply, shift=outer * p_next, axis=0)  6.57 us
  transfers between devices with their start and end apart: 3, of which 3 were waited for; matrix products, arithmetic and copies ran while one was open for 0% of the time, Pallas kernels for 0%

profile of v1, /device:TPU:5, one launch (start us, length us, event | category | flops | bytes accessed | tf_op | source)
XLA Modules:
  0.0 220.7 jit_solution(1683710784332595914)
XLA Ops:
  0.0 1.2 collective-permute-start
  1.2 15.0 %collective-permute-done = bf16[10,2,12,1408]{3,1,2,0:T(2,128)(2,1)S(1)} collective-permute-done((bf16[10,2,12,1408]{3,1,2,0:T(2,128)(2,1)}, bf16[10,2,12,1408]{3,1,2,0:T(2,128)(2,1)S(1)}, u32[]{:S(2)}, u32[]{:S(2)}) %collective-permute-start) | collective-permute-done | bytes 675872 | tf_op jit(solution)/shard_map/ppermute | solution.py:65
  16.3 6.6 %fusion.9 = bf16[20,2,12,1408]{3,1,2,0:T(2,128)(2,1)S(1)} fusion(s32[]{:T(128)S(6)} %select_n.18, bf16[10,2,12,1408]{3,1,2,0:T(2,128)(2,1)S(1)} %collective-permute-done, bf16[10,2,12,1408]{3,1,2,0:T(2,128)(2,1)} %param.1), kind=kLoop, calls=%fused_computation.18 | loop fusion | flops 2027520 | bytes 2703364 | tf_op jit(solution)/shard_map/jit(_roll_dynamic)/concatenate | solution.py:67
  22.8 0.5 fusion.17
  23.3 4.6 %collective-permute-start.1 = (bf16[20,2,3,1408]{3,1,2,0:T(2,128)(2,1)S(1)}, bf16[20,2,3,1408]{3,1,2,0:T(2,128)(2,1)S(1)}, u32[]{:S(2)}, u32[]{:S(2)}) collective-permute-start(bf16[20,2,3,1408]{3,1,2,0:T(2,128)(2,1)S(1)} %get-tuple-element.9), channel_id=1, source_target_pairs={{0,1},{1,2},{2,3},{3,4},{4,5},{5,6},{6,7},{7,8},{8,9},{9,10},{10,1... | collective-permute-start | bytes 1013768 | tf_op jit(solution)/shard_map/ppermute | solution.py:17
  27.9 1.9 collective-permute-start.2
  29.8 2.2 collective-permute-done.1
  32.0 5.3 %collective-permute-done.2 = bf16[20,2,3,1408]{3,1,2,0:T(2,128)(2,1)S(1)} collective-permute-done((bf16[20,2,3,1408]{3,1,2,0:T(2,128)(2,1)S(1)}, bf16[20,2,3,1408]{3,1,2,0:T(2,128)(2,1)S(1)}, u32[]{:S(2)}, u32[]{:S(2)}) %collective-permute-start.2) | collective-permute-done | bytes 337952 | tf_op jit(solution)/shard_map/ppermute | solution.py:19
  37.3 6.8 %multiply_reduce_fusion = (f32[20,18,1408]{2,1,0:T(8,128)S(1)}, bf16[20,2,18,1408]{3,1,2,0:T(2,128)(2,1)}) fusion(bf16[20,2,3,1408]{3,1,2,0:T(2,128)(2,1)S(1)} %collective-permute-done.2, bf16[20,2,12,1408]{3,1,2,0:T(2,128)(2,1)S(1)} %fusion.9, bf16[20,2,3,1408]{3,1,2,0:T(2,128)(2,1)S(1)} %collective-permute-done.1), kind=kLoop, calls=%fused_computation.8 | loop fusion | flops 4561920 | bytes 6082560 | tf_op jit(solution)/shard_map/reduce_sum | solution.py:39
  44.1 0.4 copy.15
  44.5 26.0 %reduce_sum.14 = f32[20,6,3,128,11]{4,3,0,2,1:T(8,128)} reshape(f32[20,18,1408]{2,0,1:T(8,128)S(1)} %copy.15) | data formatting | bytes 4055040 | tf_op jit(solution)/shard_map/reduce_sum | solution.py:39
  70.5 0.0 copy-start
  70.5 9.4 %reduce_sum.18 = f32[20,6,128]{2,0,1:T(8,128)S(1)} reduce(f32[20,6,3,128,11]{4,3,0,2,1:T(8,128)} %reduce_sum.14, f32[]{:T(128)} %constant.32.clone.1), dimensions={2,4}, to_apply=%region_1.2 | reduce | flops 491520 | bytes 2088964 | tf_op jit(solution)/shard_map/reduce_sum | solution.py:39
  80.0 0.1 fusion.14
  80.2 0.0 copy-done
  80.2 54.0 %reshape.43 = bf16[20,2,6,3,128,11]{5,4,1,3,2,0:T(8,128)(2,1)} reshape(bf16[20,2,18,1408]{3,1,2,0:T(2,128)(2,1)S(1)} %copy-done) | data formatting | bytes 4055040 | tf_op jit(solution)/shard_map/reshape | solution.py:28
  134.2 11.3 %constant_dynamic-slice_fusion.1 = bf16[10,2,6,3,128,11]{5,4,1,3,2,0:T(8,128)(2,1)} fusion(bf16[20,2,6,3,128,11]{5,4,1,3,2,0:T(8,128)(2,1)} %reshape.43, s32[]{:T(128)S(6)} %select_n.19), kind=kLoop, calls=%fused_computation.35 | loop fusion | bytes 2027524 | tf_op jit(solution)/shard_map/dynamic_slice | solution.py:72
  145.5 45.5 %fusion.2 = f32[6,128,10,2,20,2]{4,2,5,3,1,0:T(8,128)} fusion(bf16[20,2,6,3,128,11,1]{5,4,1,3,2,0,6:T(8,128)(2,1)} %bitcast.21, bf16[10,2,6,3,128,11]{5,4,1,3,2,0:T(8,128)(2,1)} %constant_dynamic-slice_fusion.1), kind=kOutput, calls=%fused_computation.3 | convolution fusion | flops 40550400 | bytes 5498880 | tf_op jit(solution)/shard_map/dot_general | solution.py:44
  190.9 14.1 %fusion.6 = (f32[6,128,10,20,1]{3,2,1,0,4:T(8,128)}, f32[6,128,10,20,1]{3,2,1,0,4:T(8,128)}) fusion(f32[6,128,10,2,20,2]{4,2,5,3,1,0:T(8,128)} %fusion.2), kind=kLoop, calls=%fused_computation.7 | loop fusion | flops 307200 | bytes 3686400 | tf_op jit(solution)/shard_map/add | solution.py:50
  205.1 5.0 %copy.13 = f32[6,128,10,20,1]{1,4,3,2,0:T(1,128)S(1)} copy(f32[6,128,10,20,1]{3,2,1,0,4:T(8,128)} %get-tuple-element.7) | data formatting | bytes 1228800 | tf_op jit(solution)/shard_map/add | solution.py:50
  210.0 5.2 %copy.14 = f32[6,128,10,20,1]{1,4,3,2,0:T(1,128)S(1)} copy(f32[6,128,10,20,1]{3,2,1,0,4:T(8,128)} %get-tuple-element.8) | data formatting | bytes 1228800 | tf_op jit(solution)/shard_map/sub | solution.py:51
  215.2 1.1 maximum_bitcast_fusion
  216.4 2.6 %fusion.11 = f32[10,20,2,6,128]{4,2,1,0,3:T(2,128)S(1)} fusion(f32[10,20,2,6,128]{4,2,1,0,3:T(2,128)S(1)} %maximum_bitcast_fusion), kind=kLoop, calls=%fused_computation.20 | loop fusion | flops 614400 | bytes 2457600 | tf_op jit(solution)/shard_map/add | solution.py:33
  219.0 0.5 fusion.12
  219.5 1.2 copy.16
  (3 shorter events, 0.1 us)
Async XLA Ops:
  0.0 16.2 %collective-permute-start = (bf16[10,2,12,1408]{3,1,2,0:T(2,128)(2,1)}, bf16[10,2,12,1408]{3,1,2,0:T(2,128)(2,1)S(1)}, u32[]{:S(2)}, u32[]{:S(2)}) collective-permute-start(bf16[10,2,12,1408]{3,1,2,0:T(2,128)(2,1)} %param.1), channel_id=1, source_target_pairs={{0,16},{16,0},{1,17},{17,1},{2,18},{18,2},{3,19},{19,3},{4,20},{20... | collective-permute-start | bytes 2027528 | tf_op jit(solution)/shard_map/ppermute | solution.py:65
  23.3 8.7 %collective-permute-start.1 = (bf16[20,2,3,1408]{3,1,2,0:T(2,128)(2,1)S(1)}, bf16[20,2,3,1408]{3,1,2,0:T(2,128)(2,1)S(1)}, u32[]{:S(2)}, u32[]{:S(2)}) collective-permute-start(bf16[20,2,3,1408]{3,1,2,0:T(2,128)(2,1)S(1)} %get-tuple-element.9), channel_id=1, source_target_pairs={{0,1},{1,2},{2,3},{3,4},{4,5},{5,6},{6,7},{7,8},{8,9},{9,10},{10,1... | collective-permute-start | bytes 1013768 | tf_op jit(solution)/shard_map/ppermute | solution.py:17
  27.9 9.4 %collective-permute-start.2 = (bf16[20,2,3,1408]{3,1,2,0:T(2,128)(2,1)S(1)}, bf16[20,2,3,1408]{3,1,2,0:T(2,128)(2,1)S(1)}, u32[]{:S(2)}, u32[]{:S(2)}) collective-permute-start(bf16[20,2,3,1408]{3,1,2,0:T(2,128)(2,1)S(1)} %get-tuple-element.10), channel_id=1, source_target_pairs={{1,0},{2,1},{3,2},{4,3},{5,4},{6,5},{7,6},{8,7},{9,8},{10,9},{11,1... | collective-permute-start | bytes 1013768 | tf_op jit(solution)/shard_map/ppermute | solution.py:19
  70.5 9.6 %copy-start = (bf16[20,2,18,1408]{3,1,2,0:T(2,128)(2,1)S(1)}, bf16[20,2,18,1408]{3,1,2,0:T(2,128)(2,1)}, u32[]{:S(2)}) copy-start(bf16[20,2,18,1408]{3,1,2,0:T(2,128)(2,1)} %get-tuple-element.6) | copy-start | bytes 6082564
